TPU v7x, 32 devices: a whole 2x2x4 slice. The times are simulated.
32 devices in a mesh: rows: 8 (over y, x, core), draws: 4 (over z).
Axes of the slice: x: 2, y: 2, z: 4, core: 2. Of those that a mesh axis runs over, the one named last changes fastest.
Arguments:
- pool_inputs: bfloat16 [2048, 4096], P('rows', 'draws'), may hold values from -8 to 8
- target_inputs: bfloat16 [2048, 4096], P('rows', 'draws'), may hold values from -8 to 8
- class_weights: bfloat16 [4096, 4096], P(None, 'draws'), may hold values from -1 to 1
- class_bias: float32 [4096], P('draws'), may hold values from -6 to 6
Outputs:
- gain: float32 [2048], P('rows')
All inputs are finite; a program needn't handle non-finite values.
Results may differ from a plain program's by a relative error of at most 0.003.
Values may be sent and summed in bfloat16 or wider, within the bound.
A program may use at most 64 MiB of HBM per device.

v0:
```python
import math

import jax
import jax.numpy as jnp
from jax import lax
from jax.sharding import PartitionSpec as P

C = 16


def head_probs(logits, class_bias, count, heads):
    probs = jax.nn.softmax((logits + class_bias).reshape(count, heads, C), axis=-1)
    return jnp.transpose(probs, (1, 0, 2)).reshape(heads, count * C).astype(jnp.bfloat16)


def entropy_of(probs, count):
    ones = jnp.ones((probs.shape[0],), jnp.bfloat16)
    mean = (jnp.dot(ones, probs, preferred_element_type=jnp.float32) / probs.shape[0]).reshape(
        count, C
    )
    return -jnp.sum(jax.scipy.special.xlogy(mean, mean), axis=-1)


def local(pool_inputs, target_inputs, class_weights, class_bias):
    pool_count = pool_inputs.shape[0]
    target_count = target_inputs.shape[0]
    columns = class_weights.shape[1]
    heads = columns // C
    pool_logits = jnp.dot(
        lax.all_gather(pool_inputs, "draws", axis=1, tiled=True),
        class_weights,
        preferred_element_type=jnp.float32,
    )
    target_logits = jnp.dot(
        lax.all_gather(target_inputs, "draws", axis=1, tiled=True),
        class_weights,
        preferred_element_type=jnp.float32,
    )
    pool_local = head_probs(pool_logits, class_bias, pool_count, heads)
    target_local = head_probs(target_logits, class_bias, target_count, heads)
    pool_probs = lax.all_gather(pool_local, "draws", axis=0, tiled=True)
    partner_part = lax.all_to_all(target_local, "draws", split_axis=1, concat_axis=0, tiled=True)
    target_probs = lax.all_gather(partner_part, "rows", axis=1, tiled=True)
    all_heads = pool_probs.shape[0]
    paired = target_probs.shape[1] // C
    pool_entropy = entropy_of(pool_probs, pool_count)
    target_entropy = entropy_of(target_probs, paired)
    block = math.gcd(paired, 32)

    def add_block(index, total):
        piece = lax.dynamic_slice_in_dim(target_probs, index * block * C, block * C, 1)
        joint = (
            lax.dot_general(
                pool_probs, piece, (((0,), (0,)), ((), ())), preferred_element_type=jnp.float32
            )
            / all_heads
        )
        joint = joint.reshape(pool_count, C, block, C)
        return total + jnp.sum(jax.scipy.special.xlogy(joint, joint), axis=(1, 2, 3))

    partial_sum = lax.fori_loop(
        0, paired // block, add_block, jnp.zeros((pool_count,), jnp.float32)
    )
    partial_sum = partial_sum + jnp.sum(target_entropy)
    total = lax.psum(partial_sum, "draws")
    return total / (paired * lax.axis_size("draws")) + pool_entropy


def solution(mesh):
    placed = (P("rows", "draws"), P("rows", "draws"), P(None, "draws"), P("draws"))
    return jax.shard_map(local, mesh=mesh, in_specs=placed, out_specs=P("rows"), check_vma=False)
```

profile of v0, /device:TPU:0, one launch (start us, length us, event | category | flops | bytes accessed | tf_op | source)
XLA Modules:
  0.0 293.2 jit_solution(697630218376808612)
XLA Ops:
  6.5 0.7 all-gather.9.cloned.1.call-update
  7.3 0.7 all-gather.5.cloned.1.call-update
  8.1 49.3 %all-gather.9.cloned.1.call-done = bf16[256,4096]{1,0:T(8,128)(2,1)} async-done(((bf16[256,1024]{1,0:T(8,128)(2,1)}), bf16[256,4096]{1,0:T(8,128)(2,1)}) %all-gather.9.cloned.1.call-update) | async-done | bytes 2097168 | tf_op jit(solution)/shard_map/all_gather | solution.py:30
  57.3 6.3 %convolution_add_fusion = f32[256,1024]{1,0:T(8,128)S(1)} fusion(bf16[256,4096]{1,0:T(8,128)(2,1)} %all-gather.9.cloned.1.call-done, bf16[4096,1024]{1,0:T(8,128)(2,1)} %param.8, f32[1024]{0:T(1024)} %param.9), kind=kOutput, calls=%fused_computation.19 | convolution fusion | flops 2147745792 | bytes 11538432 | tf_op jit(solution)/shard_map/dot_general | solution.py:29
  63.6 0.3 copy.20
  64.0 0.4 fusion.18
  64.4 1.3 copy.21
  65.7 1.1 copy.22
  66.9 36.5 %all-gather.5.cloned.1.call-done = bf16[256,4096]{1,0:T(8,128)(2,1)} async-done(((bf16[256,1024]{1,0:T(8,128)(2,1)}), bf16[256,4096]{1,0:T(8,128)(2,1)}) %all-gather.5.cloned.1.call-update) | async-done | bytes 2097168 | tf_op jit(solution)/shard_map/all_gather | solution.py:35
  103.4 6.3 %convolution_add_fusion.1 = f32[256,1024]{1,0:T(8,128)S(1)} fusion(bf16[256,4096]{1,0:T(8,128)(2,1)} %all-gather.5.cloned.1.call-done, bf16[4096,1024]{1,0:T(8,128)(2,1)} %param.8, f32[1024]{0:T(1024)S(1)} %copy-done.1), kind=kOutput, calls=%fused_computation.20 | convolution fusion | flops 2147745792 | bytes 11538432 | tf_op jit(solution)/shard_map/dot_general | solution.py:34
  109.7 0.3 copy.17
  110.1 0.4 fusion.17
  110.5 1.3 copy.18
  111.8 0.3 copy.19
  112.1 32.4 %all_to_all.16 = bf16[64,4,1024]{2,0,1:T(8,128)(2,1)} all-to-all(bf16[64,4,1024]{2,0,1:T(8,128)(2,1)S(1)} %copy.19), channel_id=1, replica_groups=mesh['rows'=8,'draws'=4] {'draws'}, dimensions={1} | all-to-all | bytes 1048576 | tf_op jit(solution)/shard_map/all_to_all | solution.py:42
  144.5 16.1 %all-gather.11.cloned.1.call-done = bf16[256,4096]{1,0:T(8,128)(2,1)} async-done(((bf16[64,4096]{1,0:T(8,128)(2,1)}), bf16[256,4096]{1,0:T(8,128)(2,1)}) %all-gather.11.cloned.1.call-update) | async-done | bytes 2097168 | tf_op jit(solution)/shard_map/all_gather | solution.py:41
  160.7 2.1 fusion.23
  162.8 0.1 reshape.34
  162.9 0.1 fusion.20
  163.0 34.7 %all-gather.7.cloned.1.call-done = bf16[256,8192]{1,0:T(8,128)(2,1)} async-done(((bf16[256,1024]{1,0:T(8,128)(2,1)}), bf16[256,8192]{1,0:T(8,128)(2,1)}) %all-gather.7.cloned.1.call-update) | async-done | bytes 4194320 | tf_op jit(solution)/shard_map/all_gather | solution.py:43
  197.8 2.8 fusion.25
  200.6 0.6 fusion.22
  201.8 72.6 %while.16 = (s32[]{:T(128)}, f32[256]{0:T(256)S(1)}, bf16[256,8192]{1,0:T(8,128)(2,1)}, bf16[256,4096]{1,0:T(8,128)(2,1)S(1)}, s32[]{:T(128)}, /*index=5*/s32[]{:T(128)}, s32[]{:T(128)}, s32[]{:T(128)}, f32[]{:T(128)}) while((s32[]{:T(128)}, f32[256]{0:T(256)S(1)}, bf16[256,8192]{1,0:T(8,128)(2,1)}, ...), condition=%wide.region_7.8_spmd.clone, body=%wide.region_4.7_spmd.clone.sunk | while | flops 1088422144 | bytes 2429093 | solution.py:61
  201.8 4.3 %fusion.43 = f32[4096]{0:T(1024)S(1)} fusion(bf16[256,4096]{1,0:T(8,128)(2,1)S(1)} %get-tuple-element.193, bf16[256,8192]{1,0:T(8,128)(2,1)} %get-tuple-element.192, s32[]{:T(128)S(6)} %select_n.47), kind=kOutput, calls=%fused_computation.2.clone.1 | convolution fusion | flops 1088417792 | bytes 2375684 | tf_op jit(solution)/shard_map/while/body/eval_jaxpr/dot_general | solution.py:53
  206.1 0.1 reduce_sum.77
  206.2 0.1 reduce_sum.78
  206.4 4.3 %fusion.43 = f32[4096]{0:T(1024)S(1)} fusion(bf16[256,4096]{1,0:T(8,128)(2,1)S(1)} %get-tuple-element.193, bf16[256,8192]{1,0:T(8,128)(2,1)} %get-tuple-element.192, s32[]{:T(128)S(6)} %select_n.47), kind=kOutput, calls=%fused_computation.2.clone.1 | convolution fusion | flops 1088417792 | bytes 2375684 | tf_op jit(solution)/shard_map/while/body/eval_jaxpr/dot_general | solution.py:53
  210.8 0.1 reduce_sum.78
  210.9 4.3 %fusion.43 = f32[4096]{0:T(1024)S(1)} fusion(bf16[256,4096]{1,0:T(8,128)(2,1)S(1)} %get-tuple-element.193, bf16[256,8192]{1,0:T(8,128)(2,1)} %get-tuple-element.192, s32[]{:T(128)S(6)} %select_n.47), kind=kOutput, calls=%fused_computation.2.clone.1 | convolution fusion | flops 1088417792 | bytes 2375684 | tf_op jit(solution)/shard_map/while/body/eval_jaxpr/dot_general | solution.py:53
  215.3 0.1 reduce_sum.78
  215.4 4.3 %fusion.43 = f32[4096]{0:T(1024)S(1)} fusion(bf16[256,4096]{1,0:T(8,128)(2,1)S(1)} %get-tuple-element.193, bf16[256,8192]{1,0:T(8,128)(2,1)} %get-tuple-element.192, s32[]{:T(128)S(6)} %select_n.47), kind=kOutput, calls=%fused_computation.2.clone.1 | convolution fusion | flops 1088417792 | bytes 2375684 | tf_op jit(solution)/shard_map/while/body/eval_jaxpr/dot_general | solution.py:53
  219.7 0.1 reduce_sum.77
  219.8 0.1 reduce_sum.78
  220.0 4.3 %fusion.43 = f32[4096]{0:T(1024)S(1)} fusion(bf16[256,4096]{1,0:T(8,128)(2,1)S(1)} %get-tuple-element.193, bf16[256,8192]{1,0:T(8,128)(2,1)} %get-tuple-element.192, s32[]{:T(128)S(6)} %select_n.47), kind=kOutput, calls=%fused_computation.2.clone.1 | convolution fusion | flops 1088417792 | bytes 2375684 | tf_op jit(solution)/shard_map/while/body/eval_jaxpr/dot_general | solution.py:53
  224.3 0.1 reduce_sum.77
  224.4 0.1 reduce_sum.78
  224.5 4.3 %fusion.43 = f32[4096]{0:T(1024)S(1)} fusion(bf16[256,4096]{1,0:T(8,128)(2,1)S(1)} %get-tuple-element.193, bf16[256,8192]{1,0:T(8,128)(2,1)} %get-tuple-element.192, s32[]{:T(128)S(6)} %select_n.47), kind=kOutput, calls=%fused_computation.2.clone.1 | convolution fusion | flops 1088417792 | bytes 2375684 | tf_op jit(solution)/shard_map/while/body/eval_jaxpr/dot_general | solution.py:53
  228.9 0.1 reduce_sum.78
  229.1 4.3 %fusion.43 = f32[4096]{0:T(1024)S(1)} fusion(bf16[256,4096]{1,0:T(8,128)(2,1)S(1)} %get-tuple-element.193, bf16[256,8192]{1,0:T(8,128)(2,1)} %get-tuple-element.192, s32[]{:T(128)S(6)} %select_n.47), kind=kOutput, calls=%fused_computation.2.clone.1 | convolution fusion | flops 1088417792 | bytes 2375684 | tf_op jit(solution)/shard_map/while/body/eval_jaxpr/dot_general | solution.py:53
  233.3 0.1 reduce_sum.77
  233.4 0.1 reduce_sum.78
  233.6 4.3 %fusion.43 = f32[4096]{0:T(1024)S(1)} fusion(bf16[256,4096]{1,0:T(8,128)(2,1)S(1)} %get-tuple-element.193, bf16[256,8192]{1,0:T(8,128)(2,1)} %get-tuple-element.192, s32[]{:T(128)S(6)} %select_n.47), kind=kOutput, calls=%fused_computation.2.clone.1 | convolution fusion | flops 1088417792 | bytes 2375684 | tf_op jit(solution)/shard_map/while/body/eval_jaxpr/dot_general | solution.py:53
  237.9 0.1 reduce_sum.77
  238.0 0.1 reduce_sum.78
  238.1 4.3 %fusion.43 = f32[4096]{0:T(1024)S(1)} fusion(bf16[256,4096]{1,0:T(8,128)(2,1)S(1)} %get-tuple-element.193, bf16[256,8192]{1,0:T(8,128)(2,1)} %get-tuple-element.192, s32[]{:T(128)S(6)} %select_n.47), kind=kOutput, calls=%fused_computation.2.clone.1 | convolution fusion | flops 1088417792 | bytes 2375684 | tf_op jit(solution)/shard_map/while/body/eval_jaxpr/dot_general | solution.py:53
  242.5 0.1 reduce_sum.78
  242.7 4.3 %fusion.43 = f32[4096]{0:T(1024)S(1)} fusion(bf16[256,4096]{1,0:T(8,128)(2,1)S(1)} %get-tuple-element.193, bf16[256,8192]{1,0:T(8,128)(2,1)} %get-tuple-element.192, s32[]{:T(128)S(6)} %select_n.47), kind=kOutput, calls=%fused_computation.2.clone.1 | convolution fusion | flops 1088417792 | bytes 2375684 | tf_op jit(solution)/shard_map/while/body/eval_jaxpr/dot_general | solution.py:53
  247.0 0.1 reduce_sum.77
  247.1 0.1 reduce_sum.78
  247.2 4.3 %fusion.43 = f32[4096]{0:T(1024)S(1)} fusion(bf16[256,4096]{1,0:T(8,128)(2,1)S(1)} %get-tuple-element.193, bf16[256,8192]{1,0:T(8,128)(2,1)} %get-tuple-element.192, s32[]{:T(128)S(6)} %select_n.47), kind=kOutput, calls=%fused_computation.2.clone.1 | convolution fusion | flops 1088417792 | bytes 2375684 | tf_op jit(solution)/shard_map/while/body/eval_jaxpr/dot_general | solution.py:53
  251.6 0.1 reduce_sum.78
  251.7 4.3 %fusion.43 = f32[4096]{0:T(1024)S(1)} fusion(bf16[256,4096]{1,0:T(8,128)(2,1)S(1)} %get-tuple-element.193, bf16[256,8192]{1,0:T(8,128)(2,1)} %get-tuple-element.192, s32[]{:T(128)S(6)} %select_n.47), kind=kOutput, calls=%fused_computation.2.clone.1 | convolution fusion | flops 1088417792 | bytes 2375684 | tf_op jit(solution)/shard_map/while/body/eval_jaxpr/dot_general | solution.py:53
  256.0 0.1 reduce_sum.77
  256.1 0.1 reduce_sum.78
  256.3 4.3 %fusion.43 = f32[4096]{0:T(1024)S(1)} fusion(bf16[256,4096]{1,0:T(8,128)(2,1)S(1)} %get-tuple-element.193, bf16[256,8192]{1,0:T(8,128)(2,1)} %get-tuple-element.192, s32[]{:T(128)S(6)} %select_n.47), kind=kOutput, calls=%fused_computation.2.clone.1 | convolution fusion | flops 1088417792 | bytes 2375684 | tf_op jit(solution)/shard_map/while/body/eval_jaxpr/dot_general | solution.py:53
  260.7 0.1 reduce_sum.78
  260.8 4.3 %fusion.43 = f32[4096]{0:T(1024)S(1)} fusion(bf16[256,4096]{1,0:T(8,128)(2,1)S(1)} %get-tuple-element.193, bf16[256,8192]{1,0:T(8,128)(2,1)} %get-tuple-element.192, s32[]{:T(128)S(6)} %select_n.47), kind=kOutput, calls=%fused_computation.2.clone.1 | convolution fusion | flops 1088417792 | bytes 2375684 | tf_op jit(solution)/shard_map/while/body/eval_jaxpr/dot_general | solution.py:53
  265.2 0.1 reduce_sum.78
  265.4 4.3 %fusion.43 = f32[4096]{0:T(1024)S(1)} fusion(bf16[256,4096]{1,0:T(8,128)(2,1)S(1)} %get-tuple-element.193, bf16[256,8192]{1,0:T(8,128)(2,1)} %get-tuple-element.192, s32[]{:T(128)S(6)} %select_n.47), kind=kOutput, calls=%fused_computation.2.clone.1 | convolution fusion | flops 1088417792 | bytes 2375684 | tf_op jit(solution)/shard_map/while/body/eval_jaxpr/dot_general | solution.py:53
  269.8 0.1 reduce_sum.78
  269.9 4.3 %fusion.43 = f32[4096]{0:T(1024)S(1)} fusion(bf16[256,4096]{1,0:T(8,128)(2,1)S(1)} %get-tuple-element.193, bf16[256,8192]{1,0:T(8,128)(2,1)} %get-tuple-element.192, s32[]{:T(128)S(6)} %select_n.47), kind=kOutput, calls=%fused_computation.2.clone.1 | convolution fusion | flops 1088417792 | bytes 2375684 | tf_op jit(solution)/shard_map/while/body/eval_jaxpr/dot_general | solution.py:53
  274.3 0.1 reduce_sum.78
  274.4 11.7 %psum.7 = f32[256]{0:T(256)S(1)} all-reduce(f32[256]{0:T(256)S(1)} %broadcast_add_fusion), channel_id=1, replica_groups=mesh['rows'=8,'draws'=4] {'draws'}, use_global_device_ids=true, to_apply=%region_9.10 | all-reduce | flops 256 | bytes 2048 | tf_op jit(solution)/shard_map/psum | solution.py:65
  286.1 0.6 negate_add_fusion
  (38 shorter events, 1.2 us)
Async XLA Ops:
  6.5 50.8 %all-gather.9.cloned.1.call-start = ((), (), s32[]{:S(2)}) async-start(), calls=%async_computation.3 | async-start | bytes 2621440 | tf_op jit(solution)/shard_map/all_gather | solution.py:30
  7.3 96.1 %all-gather.5.cloned.1.call-start = ((), (), s32[]{:S(2)}) async-start(), calls=%async_computation.1 | async-start | bytes 2621440 | tf_op jit(solution)/shard_map/all_gather | solution.py:35
  8.0 152.7 %all-gather.11.cloned.1.call-start = ((), (), s32[]{:S(2)}) async-start(), calls=%async_computation.4 | async-start | bytes 2621440 | tf_op jit(solution)/shard_map/all_gather | solution.py:41
  64.0 39.4 %copy-start.1 = (f32[1024]{0:T(1024)S(1)}, f32[1024]{0:T(1024)}, u32[]{:S(2)}) copy-start(f32[1024]{0:T(1024)} %param.9) | copy-start | bytes 12292
  66.9 130.9 %all-gather.7.cloned.1.call-start = ((), (), s32[]{:S(2)}) async-start(), calls=%async_computation.2 | async-start | bytes 4718592 | tf_op jit(solution)/shard_map/all_gather | solution.py:43
  160.7 41.1 %copy-start = (bf16[256,4096]{1,0:T(8,128)(2,1)S(1)}, bf16[256,4096]{1,0:T(8,128)(2,1)}, u32[]{:S(2)}) copy-start(bf16[256,4096]{1,0:T(8,128)(2,1)} %all-gather.11.cloned.1.call-done) | copy-start | bytes 6291460
Sparse Core Ops, SparseCore 0:
  8.9 48.3 all-gather.8
  58.9 44.4 all-gather.4
  105.0 55.6 all-gather.10
  162.4 35.2 all-gather.6
where the time goes:
time: 294 us; the launch traced here: 293 us
  waiting for transfers between devices  138 us (47%)
  matrix products  86.2 us (29%)
  blocking collectives  44.1 us (15%)
  between operations  13.8 us (5%)
  local copies, waits for them, and re-layouts  6.27 us (2%)
  other arithmetic  4.08 us (1%)
    dot_general x16, matrix products, add_block(): lax.dot_general(pool_probs, piece, (((0,), (0,)), ((), ())), preferred_el...  68.6 us
    all_gather x1, waiting for transfers between devices, local(): lax.all_gather(pool_inputs, 'draws', axis=1, tiled=True)  49.3 us
    all_gather x1, waiting for transfers between devices, local(): lax.all_gather(target_inputs, 'draws', axis=1, tiled=True)  36.5 us
    all_gather x1, waiting for transfers between devices, local(): target_probs = lax.all_gather(partner_part, 'rows', axis=1, tiled=True)  34.7 us
    all_to_all x1, blocking collectives, local(): lax.all_to_all(target_local, 'draws', split_axis=1, concat_axis=0, tiled=...  32.4 us
    all_gather x1, waiting for transfers between devices, local(): pool_probs = lax.all_gather(pool_local, 'draws', axis=0, tiled=True)  16.1 us
    psum x1, blocking collectives, local(): total = lax.psum(partial_sum, 'draws')  11.7 us
    dot_general x1, matrix products, local(): jnp.dot(lax.all_gather(target_inputs, 'draws', axis=1, tiled=True), class...  6.35 us
  transfers between devices with their start and end apart: 4, of which 4 were waited for; matrix products, arithmetic and copies ran while one was open for 7% of the time, Pallas kernels for 0%

commit v1 on v0

v1 whole, which is shorter than its diff:
```python
import functools

import jax
import jax.numpy as jnp
from jax import lax
from jax.experimental import pallas as pl
from jax.experimental.pallas import tpu as pltpu
from jax.sharding import PartitionSpec as P

C = 16
LANES = 128
MESH = pl.DeviceIdType.MESH
TINY = 1.1754944e-38


def xlogx(value):
    return value * jnp.log(jnp.maximum(value, TINY))


def kernel(
    R, D, pool_ref, target_ref, weights_ref, bias_ref, out_ref,
    w, gx, logits, turned, target_local, pool_full, pool_turned, target_full,
    joint_sum, totals, stage, final,
    in_sem, f_send, f_recv, a_send, a_recv, r_send, r_recv, c_send, c_recv,
    p_send, p_recv, l_sem, t_send, t_recv,
):
    r = lax.axis_index("rows")
    z = lax.axis_index("draws")
    rows, depth = gx.shape[2], gx.shape[3]
    columns = w.shape[1]
    heads = columns // C
    K = heads * D
    part = rows // D
    fold = LANES // part
    groups = C // fold
    halves = rows // LANES
    partner = r + 1 - 2 * lax.rem(r, 2)
    pairs = R // 2
    has_right = z < D - 1
    has_left = z > 0

    inputs = (target_ref, pool_ref)

    def load(a):
        return pltpu.make_async_copy(inputs[a], gx.at[a, z], in_sem.at[a])

    load_w = pltpu.make_async_copy(weights_ref, w, in_sem.at[2])
    load(0).start()
    load(1).start()
    load_w.start()

    barrier = pltpu.get_barrier_semaphore()
    for j in range(1, D):
        pl.semaphore_signal(barrier, inc=1, device_id=(r, lax.rem(z + j, D)), device_id_type=MESH)
    for j in range(1, pairs):
        pl.semaphore_signal(barrier, inc=1, device_id=(lax.rem(r + 2 * j, R), z), device_id_type=MESH)
    pl.semaphore_signal(barrier, inc=1, device_id=(partner, z), device_id_type=MESH)
    pl.semaphore_wait(barrier, D - 1 + pairs)

    def feature(a, way, hop, owner):
        return pltpu.make_async_remote_copy(
            src_ref=gx.at[a, owner],
            dst_ref=gx.at[a, owner],
            send_sem=f_send.at[a, way, hop],
            recv_sem=f_recv.at[a, way, hop],
            device_id=(r, z + 1 - 2 * way),
            device_id_type=MESH,
        )

    def share(j):
        there = lax.rem(z + j, D)
        return pltpu.make_async_remote_copy(
            src_ref=target_local.at[there],
            dst_ref=target_full.at[r, :, pl.ds(pl.multiple_of(z * heads, heads), heads), :],
            send_sem=a_send.at[j - 1],
            recv_sem=a_recv.at[j - 1],
            device_id=(r, there),
            device_id_type=MESH,
        )

    def share_in(j):
        there = lax.rem(z + D - j, D)
        at = pl.ds(pl.multiple_of(there * heads, heads), heads)
        return pltpu.make_async_remote_copy(
            src_ref=target_local.at[there],
            dst_ref=target_full.at[r, :, at, :],
            send_sem=a_send.at[j - 1],
            recv_sem=a_recv.at[j - 1],
            device_id=(r, there),
            device_id_type=MESH,
        )

    def share_own():
        return pltpu.make_async_copy(
            target_local.at[z],
            target_full.at[r, :, pl.ds(pl.multiple_of(z * heads, heads), heads), :],
            l_sem.at[0],
        )

    def across(j, piece, there):
        return pltpu.make_async_remote_copy(
            src_ref=target_full.at[piece],
            dst_ref=target_full.at[piece],
            send_sem=r_send.at[j - 1],
            recv_sem=r_recv.at[j - 1],
            device_id=(there, z),
            device_id_type=MESH,
        )

    def beside(j, piece):
        return pltpu.make_async_remote_copy(
            src_ref=target_full.at[piece],
            dst_ref=target_full.at[piece],
            send_sem=c_send.at[j],
            recv_sem=c_recv.at[j],
            device_id=(partner, z),
            device_id_type=MESH,
        )

    def pool_copy(way, hop, owner, chunk):
        at = pl.ds(pl.multiple_of(owner * heads, heads), heads)
        return pltpu.make_async_remote_copy(
            src_ref=pool_full.at[chunk, :, at, :],
            dst_ref=pool_full.at[chunk, :, at, :],
            send_sem=p_send.at[way, hop, chunk],
            recv_sem=p_recv.at[way, hop, chunk],
            device_id=(r, z + 1 - 2 * way),
            device_id_type=MESH,
        )

    wide = min(columns, 256)

    def multiply(a, owner, first):
        base = pl.multiple_of(owner * depth, depth)

        def tile(j, carry):
            at = pl.ds(pl.multiple_of(j * wide, wide), wide)
            product = jnp.dot(
                gx[a, owner], w[pl.ds(base, depth), at], preferred_element_type=jnp.float32
            )
            if first:
                logits[:, at] = product + bias_ref[:, at]
            else:
                logits[:, at] += product
            return carry

        lax.fori_loop(0, columns // wide, tile, 0)

    lane = lax.broadcasted_iota(jnp.int32, (16, LANES), 1)
    segment = lax.div(lane, part)

    def probabilities(store):
        def turn(j, carry):
            at = pl.ds(pl.multiple_of(j * LANES, LANES), LANES)
            for h in range(halves):
                turned[h, at, :] = logits[h * LANES : (h + 1) * LANES, at].T
            return carry

        lax.fori_loop(0, columns // LANES, turn, 0)

        def some(k, carry):
            for h in range(halves):
                values = [
                    turned[h, pl.ds(k * 16 * C + c, 16, stride=C), :] for c in range(C)
                ]
                top = functools.reduce(jnp.maximum, values)
                values = [jnp.exp(v - top) for v in values]
                scale = 1.0 / functools.reduce(jnp.add, values)
                values = [v * scale for v in values]
                for g in range(groups):
                    for q in range(fold):
                        mixed = values[g * fold]
                        if q:
                            mixed = pltpu.roll(mixed, (LANES - q * part) % LANES, 1)
                        for j in range(1, fold):
                            other = values[g * fold + j]
                            shift = ((j - q) * part) % LANES
                            if shift:
                                other = pltpu.roll(other, shift, 1)
                            mixed = jnp.where(segment == j, other, mixed)
                        store(h * fold + q, g, pl.multiple_of(k * 16, 16), mixed.astype(jnp.bfloat16))
            return carry

        lax.fori_loop(0, heads // 16, some, 0)

    def store_target(chunk, g, k, value):
        target_local[chunk, g, pl.ds(k, 16), :] = value

    def store_pool(chunk, g, k, value):
        pool_full[chunk, g, pl.ds(pl.multiple_of(z * heads + k, 16), 16), :] = value

    def start_own(a):
        @pl.when(has_right)
        def _():
            feature(a, 0, 0, z).start()

        @pl.when(has_left)
        def _():
            feature(a, 1, 0, z).start()

    def gather_step(a, s):
        @pl.when(z - s >= 0)
        def _():
            feature(a, 0, s - 1, z - s).wait_recv()

            @pl.when(has_right)
            def _():
                feature(a, 0, s, z - s).start()

        @pl.when(z + s <= D - 1)
        def _():
            feature(a, 1, s - 1, z + s).wait_recv()

            @pl.when(has_left)
            def _():
                feature(a, 1, s, z + s).start()

    def multiply_step(a, s):
        @pl.when(z - s >= 0)
        def _():
            multiply(a, z - s, False)

        @pl.when(z + s <= D - 1)
        def _():
            multiply(a, z + s, False)

    load(0).wait()
    start_own(0)
    load(1).wait()

    def start_pool(s):
        @pl.when((s == z) & has_right)
        def _():
            feature(1, 0, 0, z).start()

        @pl.when((s == D - 1 - z) & has_left)
        def _():
            feature(1, 1, 0, z).start()

    start_pool(0)
    load_w.wait()
    multiply(0, z, True)

    def target_step(s, carry):
        gather_step(0, s)
        start_pool(s)
        multiply_step(0, s)
        return carry

    lax.fori_loop(1, D, target_step, 0)
    probabilities(store_target)
    multiply(1, z, True)
    share_own().start()
    for j in range(1, D):
        share(j).start()

    def pool_step(s, carry):
        gather_step(1, s)
        multiply_step(1, s)

        @pl.when(s == max(1, D - 2))
        def _():
            share_own().wait()
            for j in range(1, D):
                share_in(j).wait_recv()
            for j in range(1, pairs):
                across(j, r, lax.rem(r + 2 * j, R)).start()
            beside(0, r).start()

        return carry

    lax.fori_loop(1, D, pool_step, 0)
    probabilities(store_pool)

    ones = jnp.ones((8, K), jnp.bfloat16)

    def fold_lanes(row):
        total = row
        for j in range(1, fold):
            total = total + pltpu.roll(row, j * part, 1)
        return total

    def entropy_rows(ref, first):
        def add(g, carry):
            mean = jnp.dot(ones, ref[first, g], preferred_element_type=jnp.float32) * (1.0 / K)
            return carry + xlogx(mean)

        return lax.fori_loop(0, groups, add, jnp.zeros((8, LANES), jnp.float32))

    def joint(chunk):
        def turn(g, carry):
            block = pool_full[chunk, g].T.astype(jnp.float32) * (1.0 / K)
            pool_turned[pl.ds(pl.multiple_of(g * LANES, LANES), LANES), :] = block.astype(
                jnp.bfloat16
            )
            return carry

        lax.fori_loop(0, groups, turn, 0)
        joint_sum[...] = jnp.zeros_like(joint_sum)
        double = 2 if groups % 2 == 0 else 1
        tall = min(256, groups * LANES)

        def column(i, carry):
            piece = lax.div(i, groups // double)
            g = lax.rem(i, groups // double) * double
            block = jnp.concatenate([target_full[piece, g + b] for b in range(double)], axis=1)
            total = None
            for top in range(0, groups * LANES, tall):
                value = xlogx(
                    jnp.dot(
                        pool_turned[top : top + tall, :], block, preferred_element_type=jnp.float32
                    )
                )
                for u in range(0, tall, LANES):
                    for v in range(0, double * LANES, LANES):
                        term = value[u : u + LANES, v : v + LANES]
                        total = term if total is None else total + term
            joint_sum[...] += total
            return carry

        lax.fori_loop(0, R * groups // double, column, 0)
        summed = jnp.sum(joint_sum[...].T, axis=0, keepdims=True)
        totals[0, chunk] = fold_lanes(jnp.broadcast_to(summed, (8, LANES)))
        totals[1, chunk] = fold_lanes(entropy_rows(pool_full, chunk))

    def finish_targets():
        for j in range(1, pairs):
            piece = lax.rem(r + R - 2 * j, R)
            across(j, piece, piece).wait_recv()
            beside(j, piece).start()
        for j in range(pairs):
            beside(j, lax.rem(partner + R - 2 * j, R)).wait_recv()

    def pool_round(t, carry):
        for s in range(D):
            chunk = t - s
            valid = (chunk >= 0) & (chunk < D)

            @pl.when(valid & (z - s >= 0))
            def _():
                if s:
                    pool_copy(0, s - 1, z - s, chunk).wait_recv()
                if s < D - 1:
                    @pl.when(has_right)
                    def _():
                        pool_copy(0, s, z - s, chunk).start()

            @pl.when(valid & (z + s <= D - 1))
            def _():
                if s:
                    pool_copy(1, s - 1, z + s, chunk).wait_recv()
                if s < D - 1:
                    @pl.when(has_left)
                    def _():
                        pool_copy(1, s, z + s, chunk).start()

        @pl.when(t == D - 1)
        def _():
            finish_targets()

        @pl.when(t >= D - 1)
        def _():
            joint(t - (D - 1))

        return carry

    lax.fori_loop(0, 2 * D - 1, pool_round, 0)

    def target_entropy(piece, carry):
        return carry + entropy_rows(target_full, piece)

    sums = lax.fori_loop(0, R, target_entropy, jnp.zeros((8, LANES), jnp.float32))
    targets_sum = jnp.sum(sums) * 0.125

    seg8 = lax.div(lax.broadcasted_iota(jnp.int32, (8, LANES), 1), part)

    def laid(which, h):
        row = totals[which, h * fold]
        for q in range(1, fold):
            row = jnp.where(seg8 == q, totals[which, h * fold + q], row)
        return row

    for h in range(halves):
        stage[h] = laid(0, h) - targets_sum
    keep = pltpu.make_async_copy(stage, final.at[z], l_sem.at[1])
    keep.start()
    keep.wait()

    def total_copy(j, owner, there):
        return pltpu.make_async_remote_copy(
            src_ref=final.at[owner],
            dst_ref=final.at[owner],
            send_sem=t_send.at[j - 1],
            recv_sem=t_recv.at[j - 1],
            device_id=(r, there),
            device_id_type=MESH,
        )

    for j in range(1, D):
        total_copy(j, z, lax.rem(z + j, D)).start()

    def ended(s, carry):
        for a in range(2):
            @pl.when((z - s >= 0) & has_right)
            def _():
                feature(a, 0, s, z - s).wait_send()

            @pl.when((z + s <= D - 1) & has_left)
            def _():
                feature(a, 1, s, z + s).wait_send()

        for chunk in range(D):
            @pl.when((z - s >= 0) & has_right)
            def _():
                pool_copy(0, s, z - s, chunk).wait_send()

            @pl.when((z + s <= D - 1) & has_left)
            def _():
                pool_copy(1, s, z + s, chunk).wait_send()

        return carry

    lax.fori_loop(0, D - 1, ended, 0)
    for j in range(1, D):
        share(j).wait_send()
    for j in range(1, pairs):
        across(j, r, lax.rem(r + 2 * j, R)).wait_send()
    for j in range(pairs):
        beside(j, lax.rem(r + R - 2 * j, R)).wait_send()
    for j in range(1, D):
        there = lax.rem(z + D - j, D)
        total_copy(j, there, there).wait_recv()
    for j in range(1, D):
        total_copy(j, z, lax.rem(z + j, D)).wait_send()
    scale = 1.0 / (R * part * D)
    for h in range(halves):
        total = final[0, h]
        for d in range(1, D):
            total = total + final[d, h]
        out_ref[h] = total * scale - laid(1, h)


def local(R, D, pool_inputs, target_inputs, class_weights, class_bias):
    rows, depth = pool_inputs.shape
    features, columns = class_weights.shape
    heads = columns // C
    K = heads * D
    part = rows // D
    fold = LANES // part
    groups = C // fold
    halves = rows // LANES
    bf16, f32 = jnp.bfloat16, jnp.float32
    DMA = pltpu.SemaphoreType.DMA
    anywhere = pl.BlockSpec(memory_space=pl.ANY)
    out = pl.pallas_call(
        functools.partial(kernel, R, D),
        out_shape=jax.ShapeDtypeStruct((halves, 8, LANES), f32),
        in_specs=[anywhere, anywhere, anywhere, pl.BlockSpec(memory_space=pltpu.VMEM)],
        out_specs=pl.BlockSpec(memory_space=pltpu.VMEM),
        scratch_shapes=[
            pltpu.VMEM((features, columns), bf16),
            pltpu.VMEM((2, D, rows, depth), bf16),
            pltpu.VMEM((rows, columns), f32),
            pltpu.VMEM((halves, columns, LANES), f32),
            pltpu.VMEM((D, groups, heads, LANES), bf16),
            pltpu.VMEM((D, groups, K, LANES), bf16),
            pltpu.VMEM((groups * LANES, K), bf16),
            pltpu.VMEM((R, groups, K, LANES), bf16),
            pltpu.VMEM((LANES, LANES), f32),
            pltpu.VMEM((2, D, 8, LANES), f32),
            pltpu.VMEM((halves, 8, LANES), f32),
            pltpu.VMEM((D, halves, 8, LANES), f32),
            DMA((3,)),
            DMA((2, 2, D - 1)),
            DMA((2, 2, D - 1)),
            DMA((D - 1,)),
            DMA((D - 1,)),
            DMA((R // 2 - 1,)),
            DMA((R // 2 - 1,)),
            DMA((R // 2,)),
            DMA((R // 2,)),
            DMA((2, D - 1, D)),
            DMA((2, D - 1, D)),
            DMA((2,)),
            DMA((D - 1,)),
            DMA((D - 1,)),
        ],
        compiler_params=pltpu.CompilerParams(collective_id=0, has_side_effects=True),
        name="gain",
    )(pool_inputs, target_inputs, class_weights, class_bias.reshape(1, columns))
    return out[:, 0, :].reshape(rows)


def solution(mesh):
    R, D = mesh.shape["rows"], mesh.shape["draws"]
    placed = (P("rows", "draws"), P("rows", "draws"), P(None, "draws"), P("draws"))
    return jax.shard_map(
        functools.partial(local, R, D),
        mesh=mesh,
        in_specs=placed,
        out_specs=P("rows"),
        check_vma=False,
    )
```

time: 294 us -> 176 us (0.60)
  Pallas kernels: 0 us -> 172 us
  waiting for transfers between devices: 138 us -> 0 us
  matrix products: 86.2 us -> 0 us
  blocking collectives: 44.1 us -> 0 us
  between operations: 13.8 us -> 0.01 us
  local copies, waits for them, and re-layouts: 6.27 us -> 1.26 us
  other arithmetic: 4.08 us -> 0 us
    pallas_call x0 -> x1, Pallas kernels: none -> 172 us  [local(): pl.pallas_call(functools.partial(kernel, R, D), out_shape=jax.ShapeDtypeS...]
    all_gather x4 -> x0, waiting for transfers between devices: 137 us -> none  [the longest x1 49.3 us: local(): lax.all_gather(pool_inputs, 'draws', axis=1, tiled=True)]
    dot_general x20 -> x0, matrix products: 86.2 us -> none  [the longest x16 68.6 us: add_block(): lax.dot_general(pool_probs, piece, (((0,), (0,)), ((), ())), preferred_el...]
    all_to_all x1 -> x0, blocking collectives: 32.4 us -> none  [local(): lax.all_to_all(target_local, 'draws', split_axis=1, concat_axis=0, tiled=...]
    psum x1 -> x0, blocking collectives: 11.7 us -> none  [local(): total = lax.psum(partial_sum, 'draws')]
    convert_element_type x4 -> x0, local copies, waits for them, and re-layouts: 4.04 us -> none  [head_probs(): jnp.transpose(probs, (1, 0, 2)).reshape(heads, count * C)]
  transfers between devices with their start and end apart: 4 -> 0, of which waited for: 4 -> 0; matrix products, arithmetic and copies ran while one was open for 7% -> 0% of each run, Pallas kernels for 0% -> 0%
where the time goes in v1:
time: 176 us; the launch traced here: 174 us
  Pallas kernels  172 us (98%)
    pallas_call x1, Pallas kernels, local(): pl.pallas_call(functools.partial(kernel, R, D), out_shape=jax.ShapeDtypeS...  172 us

profile of v1, /device:TPU:0, one launch (start us, length us, event | category | flops | bytes accessed | tf_op | source)
XLA Modules:
  0.0 173.6 jit_solution(10355336115798735921)
XLA Ops:
  0.0 172.3 %gain.1 = f32[2,8,128]{2,1,0:T(8,128)} custom-call(bf16[256,1024]{1,0:T(8,128)(2,1)} %pool_ref.1, bf16[256,1024]{1,0:T(8,128)(2,1)} %target_ref.1, bf16[4096,1024]{1,0:T(8,128)(2,1)} %weights_ref.1, f32[1,1024]{1,0:T(1,128)} %bitcast.2), custom_call_target="tpu_custom_call" | custom-call | tf_op jit(solution)/shard_map/gain/pallas_call | solution.py:455
  172.3 1.3 slice.3

commit v2 on v1

--- a/solution.py
+++ b/solution.py
@@ -1,4 +1,5 @@
 import functools
+import math
 
 import jax
 import jax.numpy as jnp
@@ -297,8 +298,8 @@
 
         lax.fori_loop(0, groups, turn, 0)
         joint_sum[...] = jnp.zeros_like(joint_sum)
-        double = 2 if groups % 2 == 0 else 1
-        tall = min(256, groups * LANES)
+        double = math.gcd(groups, 8)
+        tall = 256
 
         def column(i, carry):
             piece = lax.div(i, groups // double)

time: 176 us -> 160 us (0.909)
  Pallas kernels: 172 us -> 156 us
    pallas_call x1, Pallas kernels: 172 us -> 156 us  [local(): pl.pallas_call(functools.partial(kernel, R, D), out_shape=jax.ShapeDtypeS...]
where the time goes in v2:
time: 160 us; the launch traced here: 158 us
  Pallas kernels  156 us (98%)
    pallas_call x1, Pallas kernels, local(): pl.pallas_call(functools.partial(kernel, R, D), out_shape=jax.ShapeDtypeS...  156 us

profile of v2, /device:TPU:0, one launch (start us, length us, event | category | flops | bytes accessed | tf_op | source)
XLA Modules:
  0.0 157.6 jit_solution(14149689003927876620)
XLA Ops:
  0.0 156.4 %gain.1 = f32[2,8,128]{2,1,0:T(8,128)} custom-call(bf16[256,1024]{1,0:T(8,128)(2,1)} %pool_ref.1, bf16[256,1024]{1,0:T(8,128)(2,1)} %target_ref.1, bf16[4096,1024]{1,0:T(8,128)(2,1)} %weights_ref.1, f32[1,1024]{1,0:T(1,128)} %bitcast.2), custom_call_target="tpu_custom_call" | custom-call | tf_op jit(solution)/shard_map/gain/pallas_call | solution.py:456
  156.4 1.3 slice.3

commit v3 on v2

--- a/solution.py
+++ b/solution.py
@@ -286,7 +286,10 @@
             mean = jnp.dot(ones, ref[first, g], preferred_element_type=jnp.float32) * (1.0 / K)
             return carry + xlogx(mean)
 
-        return lax.fori_loop(0, groups, add, jnp.zeros((8, LANES), jnp.float32))
+        total = jnp.zeros((8, LANES), jnp.float32)
+        for g in range(groups):
+            total = add(g, total)
+        return total
 
     def joint(chunk):
         def turn(g, carry):
@@ -355,9 +358,17 @@
                     def _():
                         pool_copy(1, s, z + s, chunk).start()
 
+        @pl.when(t == min(1, D - 1))
+        def _():
+            for j in range(1, pairs):
+                piece = lax.rem(r + R - 2 * j, R)
+                across(j, piece, piece).wait_recv()
+                beside(j, piece).start()
+
         @pl.when(t == D - 1)
         def _():
-            finish_targets()
+            for j in range(pairs):
+                beside(j, lax.rem(partner + R - 2 * j, R)).wait_recv()
 
         @pl.when(t >= D - 1)
         def _():

time: 160 us -> 146 us (0.912); the launches traced: 158 us -> 145 us
  Pallas kernels: 156 us -> 144 us
    pallas_call x1, Pallas kernels: 156 us -> 144 us  [local(): pl.pallas_call(functools.partial(kernel, R, D), out_shape=jax.ShapeDtypeS...]
where the time goes in v3:
time: 146 us; the launch traced here: 145 us
  Pallas kernels  144 us (99%)
    pallas_call x1, Pallas kernels, local(): pl.pallas_call(functools.partial(kernel, R, D), out_shape=jax.ShapeDtypeS...  144 us

profile of v3, /device:TPU:0, one launch (start us, length us, event | category | flops | bytes accessed | tf_op | source)
XLA Modules:
  0.0 145.5 jit_solution(6311896061556782778)
XLA Ops:
  0.0 144.2 %gain.1 = f32[2,8,128]{2,1,0:T(8,128)} custom-call(bf16[256,1024]{1,0:T(8,128)(2,1)} %pool_ref.1, bf16[256,1024]{1,0:T(8,128)(2,1)} %target_ref.1, bf16[4096,1024]{1,0:T(8,128)(2,1)} %weights_ref.1, f32[1,1024]{1,0:T(1,128)} %bitcast.2), custom_call_target="tpu_custom_call" | custom-call | tf_op jit(solution)/shard_map/gain/pallas_call | solution.py:467
  144.2 1.3 slice.3
